TPU v7x, 32 devices: a whole 2x2x4 slice. The times are simulated.
32 devices in a mesh: dp: 8 (over y, x, core), head: 4 (over z).
Axes of the slice: x: 2, y: 2, z: 4, core: 2. Of those that a mesh axis runs over, the one named last changes fastest.
Arguments:
- block_input: bfloat16 [8192, 1536], P(('dp', 'head')), may hold values from -6 to 6
- seq_lengths: int32 [32], P('dp'), may hold values from 1 to 256, 5120 in all
- cotangent: bfloat16 [8192, 1536], P(('dp', 'head')), may hold values from -6 to 6
- norm_gain: float32 [1536], replicated, may hold values from 0.5 to 1.5
- proj_zx: float32 [1536, 2, 3072], P('dp', None, 'head'), may hold values from -0.15625 to 0.15625
- proj_dt: float32 [1536, 48], P('dp', 'head'), may hold values from -0.15625 to 0.15625
- proj_bc: float32 [1536, 256], P('dp'), may hold values from -0.15625 to 0.15625
- chan_params: float32 [6, 3072], P(None, 'head'), may hold values from -2 to 2, as said below
- conv_bc: float32 [5, 256], replicated, may hold values from -3 to 3, as said below
- head_params: float32 [3, 48], P(None, 'head'), may hold values from -5 to 3.2, as said below
- out_proj: float32 [3072, 1536], P(('head', 'dp')), may hold values from -0.109375 to 0.109375
- gain_moments: float32 [2, 1536], replicated, may hold values from -40 to 40, as said below
- zx_moments: float32 [2, 1536, 2, 3072], P(None, 'dp', None, 'head'), may hold values from -40 to 40, as said below
- dt_moments: float32 [2, 1536, 48], P(None, 'dp', 'head'), may hold values from -40 to 40, as said below
- bc_moments: float32 [2, 1536, 256], P(None, 'dp'), may hold values from -40 to 40, as said below
- chan_moments: float32 [2, 6, 3072], P(None, None, 'head'), may hold values from -40 to 40, as said below
- convbc_moments: float32 [2, 5, 256], replicated, may hold values from -40 to 40, as said below
- head_moments: float32 [2, 3, 48], P(None, None, 'head'), may hold values from -40 to 40, as said below
- out_moments: float32 [2, 3072, 1536], P(None, ('head', 'dp')), may hold values from -40 to 40, as said below
Outputs:
- block_output: bfloat16 [8192, 1536], P(('dp', 'head'))
- input_grad: float32 [8192, 1536], P(('dp', 'head'))
- gain_next: float32 [1536], replicated
- gain_state: float32 [2, 1536], replicated
- zx_next: float32 [1536, 2, 3072], P('dp', None, 'head')
- zx_state: float32 [2, 1536, 2, 3072], P(None, 'dp', None, 'head')
- dt_next: float32 [1536, 48], P('dp', 'head')
- dt_state: float32 [2, 1536, 48], P(None, 'dp', 'head')
- bc_next: float32 [1536, 256], P('dp')
- bc_state: float32 [2, 1536, 256], P(None, 'dp')
- chan_next: float32 [6, 3072], P(None, 'head')
- chan_state: float32 [2, 6, 3072], P(None, None, 'head')
- convbc_next: float32 [5, 256], replicated
- convbc_state: float32 [2, 5, 256], replicated
- head_next: float32 [3, 48], P(None, 'head')
- head_state: float32 [2, 3, 48], P(None, None, 'head')
- outproj_next: float32 [3072, 1536], P(('head', 'dp'))
- outproj_state: float32 [2, 3072, 1536], P(None, ('head', 'dp'))
Inputs may be any that keep to these rules, and one draw needn't show every extreme that they name: Each padded sequence is live on its first seq_lengths positions; the lengths sum to 5120 and some sequence is live on all 256 positions. `chan_params`: taps in -2 to 2, bias in -0.5 to 0.5, gate gains in 0.5 to 1.5. `conv_bc`: taps and biases of B and C. `head_params`: A_log in -3 to 3.2, step bias in -5 to -1, skip coefficient in 0.5 to 1.5. `gain_moments`: root second moments lie in 3 to 40. `zx_moments`: root second moments lie in 3 to 40. `dt_moments`: root second moments lie in 3 to 40. `bc_moments`: root second moments lie in 3 to 40. `chan_moments`: root second moments lie in 3 to 40. `convbc_moments`: root second moments lie in 3 to 40. `head_moments`: root second moments lie in 3 to 40. `out_moments`: root second moments lie in 3 to 40.
All inputs are finite; a program needn't handle non-finite values. No bound on the sum of `seq_lengths` on one device may be relied on, other than what follows from the above.
Results may differ from a plain program's by a relative error of at most 0.012.
Values may be sent and summed in bfloat16 or wider, within the bound.
No kernel may reach another device: no remote copies, remote signals or barrier semaphores. Data moves between devices by JAX's collectives and lax.ppermute only.
A program may use at most 128 MiB of HBM per device.

v0:
```python
import jax
import jax.numpy as jnp
from jax import lax
from jax.sharding import PartitionSpec as P

norm_eps = 1e-05
beta_one = 0.9
beta_two = 0.95
adam_eps = 1e-08
step_count = 3.0
rate_matrix = 0.005
rate_vector = 0.2
weight_decay = 0.1
highest = lax.Precision.HIGHEST


def causal(values, tap_rows):
    kernel = tap_rows.shape[0] - 1
    length = values.shape[0]
    padded = jnp.pad(values, ((kernel - 1, 0), (0, 0)))
    summed = jnp.broadcast_to(tap_rows[kernel][None, :], values.shape)
    for offset in range(kernel):
        summed = summed + tap_rows[offset][None, :] * padded[offset : offset + length]
    return summed


def mixer_slot(proj_rows, bc_rows, step_raw, conv_taps, conv_shared, head_table):
    length = proj_rows.shape[0]
    inner_loc = conv_taps.shape[1]
    heads_loc = head_table.shape[1]
    headdim = inner_loc // heads_loc
    state_dim = bc_rows.shape[1] // 2
    gate_pre = proj_rows[:, :inner_loc]
    conv_x = jax.nn.silu(causal(proj_rows[:, inner_loc:], conv_taps))
    shared = jax.nn.silu(causal(bc_rows, conv_shared))
    input_map = shared[:, :state_dim]
    output_map = shared[:, state_dim:]
    step_size = jax.nn.softplus(step_raw + head_table[1][None, :])
    decay_rate = -jnp.exp(head_table[0])
    row_pos = lax.broadcasted_iota(jnp.int32, (length, length), 0)
    col_pos = lax.broadcasted_iota(jnp.int32, (length, length), 1)
    causal_mask = row_pos >= col_pos
    lower_ones = causal_mask.astype(jnp.float32)
    cum_log = jnp.dot(lower_ones, step_size * decay_rate[None, :], precision=highest).T
    log_gap = cum_log[:, :, None] - cum_log[:, None, :]
    decay_mat = jnp.exp(jnp.where(causal_mask[None], log_gap, -1e30))
    scores = jnp.dot(output_map, input_map.T, precision=highest)
    weights = scores[None] * decay_mat * step_size.T[:, None, :]
    head_values = conv_x.reshape(length, heads_loc, headdim)
    output = jnp.einsum("hts,shp->thp", weights, head_values, precision=highest)
    output = output + head_table[2][None, :, None] * head_values
    return output.reshape(length, inner_loc) * jax.nn.silu(gate_pre)


def adam_update(parameter, moments, gradient, learn_rate, decay_coef):
    first_mom = beta_one * moments[0] + (1.0 - beta_one) * gradient
    second_mom = beta_two * moments[1] * moments[1] + (1.0 - beta_two) * gradient * gradient
    second_root = jnp.sqrt(second_mom)
    first_hat = first_mom / (1.0 - beta_one**step_count)
    second_hat = second_mom / (1.0 - beta_two**step_count)
    updated = parameter - learn_rate * (
        first_hat / (jnp.sqrt(second_hat) + adam_eps) + decay_coef * parameter
    )
    return (updated, jnp.stack([first_mom, second_root]))


def shards(
    block_input,
    seq_lengths,
    cotangent,
    norm_gain,
    proj_zx,
    proj_dt,
    proj_bc,
    chan_params,
    conv_bc,
    head_params,
    out_proj,
    gain_moments,
    zx_moments,
    dt_moments,
    bc_moments,
    chan_moments,
    convbc_moments,
    head_moments,
    out_moments,
):
    slot_count = seq_lengths.shape[0]
    rows_own = block_input.shape[0]
    rows_dev = rows_own * lax.axis_size("head")
    seq_len = rows_dev // slot_count
    model_width = block_input.shape[1]
    inner_loc = chan_params.shape[1]
    inner_all = inner_loc * lax.axis_size("head")
    heads_loc = head_params.shape[1]
    kernel = chan_params.shape[0] - 2
    state_two = conv_bc.shape[1]
    row_start = lax.axis_index("head") * rows_own
    zx_full, dt_full, bc_full, out_full = (
        lax.all_gather(proj_zx.astype(jnp.bfloat16), "dp", axis=0, tiled=True),
        lax.all_gather(proj_dt.astype(jnp.bfloat16), "dp", axis=0, tiled=True),
        lax.all_gather(proj_bc.astype(jnp.bfloat16), "dp", axis=0, tiled=True),
        lax.all_gather(out_proj.astype(jnp.bfloat16), "dp", axis=0, tiled=True),
    )
    zx_mat = zx_full.reshape(model_width, 2 * inner_loc)
    positions = lax.broadcasted_iota(jnp.int32, (slot_count, seq_len), 1)
    live_mask = (positions < seq_lengths[:, None]).astype(jnp.float32).reshape(rows_dev, 1)
    live_own = lax.dynamic_slice_in_dim(live_mask, row_start, rows_own, 0)
    input_all = lax.all_gather(block_input, "head", axis=0, tiled=True)
    input_float = input_all.astype(jnp.float32)
    inv_norm = lax.rsqrt(jnp.mean(input_float * input_float, axis=-1, keepdims=True) + norm_eps)
    input_hat = input_float * inv_norm
    gain_float = lax.optimization_barrier(norm_gain.astype(jnp.bfloat16)).astype(jnp.float32)
    normed_in = (input_hat * gain_float[None, :]).astype(jnp.bfloat16)
    proj_out = jnp.dot(normed_in, zx_mat, preferred_element_type=jnp.float32)
    step_raw = jnp.dot(normed_in, dt_full, preferred_element_type=jnp.float32)
    bc_out = jnp.dot(normed_in, bc_full, preferred_element_type=jnp.float32)
    proj_slots = proj_out.reshape(slot_count, seq_len, 2 * inner_loc)
    bc_slots = bc_out.reshape(slot_count, seq_len, state_two)
    step_slots = step_raw.reshape(slot_count, seq_len, heads_loc)
    conv_taps = chan_params[: kernel + 1]
    gate_gain = chan_params[kernel + 1]

    def forward_slot(members_slot):
        return mixer_slot(
            members_slot[0], members_slot[1], members_slot[2], conv_taps, conv_bc, head_params
        )

    gated_rows = lax.map(forward_slot, (proj_slots, bc_slots, step_slots)).reshape(
        rows_dev, inner_loc
    )
    square_sum = lax.psum(jnp.sum(gated_rows * gated_rows, axis=-1), "head")
    inv_gate = lax.rsqrt(square_sum[:, None] / inner_all + norm_eps)
    normed_out = (gated_rows * inv_gate * gate_gain[None, :]).astype(jnp.bfloat16)
    branch = lax.psum_scatter(
        jnp.dot(normed_out, out_full, preferred_element_type=jnp.float32).astype(jnp.bfloat16),
        "head",
        scatter_dimension=0,
        tiled=True,
    ).astype(jnp.float32)
    block_output = (block_input.astype(jnp.float32) + live_own * branch).astype(jnp.bfloat16)
    cot_all = lax.all_gather(cotangent, "head", axis=0, tiled=True)
    cot_live = (cot_all.astype(jnp.float32) * live_mask).astype(jnp.bfloat16)
    grad_normed = jnp.dot(cot_live, out_full.T, preferred_element_type=jnp.float32)
    grad_out = jnp.dot(normed_out.T, cot_live, preferred_element_type=jnp.float32)
    grad_gate = jnp.sum(grad_normed * gated_rows * inv_gate, axis=0)
    scaled = grad_normed * gate_gain[None, :]
    cross_sum = lax.psum(jnp.sum(scaled * gated_rows, axis=-1), "head")
    grad_gated = inv_gate * scaled - gated_rows * inv_gate**3 * cross_sum[:, None] / inner_all

    def backward_slot(slot_totals, members_slot):
        unused, pullback = jax.vjp(
            mixer_slot,
            members_slot[0],
            members_slot[1],
            members_slot[2],
            conv_taps,
            conv_bc,
            head_params,
        )
        pieces = pullback(members_slot[3])
        return (
            (slot_totals[0] + pieces[3], slot_totals[1] + pieces[4], slot_totals[2] + pieces[5]),
            (pieces[0], pieces[1], pieces[2]),
        )

    zero_slot = (jnp.zeros_like(conv_taps), jnp.zeros_like(conv_bc), jnp.zeros_like(head_params))
    slot_grads, slot_cots = lax.scan(
        backward_slot,
        zero_slot,
        (proj_slots, bc_slots, step_slots, grad_gated.reshape(slot_count, seq_len, inner_loc)),
    )
    cot_proj = slot_cots[0].reshape(rows_dev, 2 * inner_loc).astype(jnp.bfloat16)
    cot_bc = slot_cots[1].reshape(rows_dev, state_two).astype(jnp.bfloat16)
    cot_step = slot_cots[2].reshape(rows_dev, heads_loc).astype(jnp.bfloat16)
    cot_input = jnp.dot(cot_proj, zx_mat.T, preferred_element_type=jnp.float32)
    cot_input = cot_input + jnp.dot(cot_step, dt_full.T, preferred_element_type=jnp.float32)
    cot_input = cot_input + jnp.dot(cot_bc, bc_full.T, preferred_element_type=jnp.float32)
    grad_zx = jnp.dot(normed_in.T, cot_proj, preferred_element_type=jnp.float32).reshape(
        model_width, 2, inner_loc
    )
    grad_dt = jnp.dot(normed_in.T, cot_step, preferred_element_type=jnp.float32)
    grad_bc = jnp.dot(normed_in.T, cot_bc, preferred_element_type=jnp.float32)
    inv_own = lax.dynamic_slice_in_dim(inv_norm, row_start, rows_own, 0)
    own_hat = block_input.astype(jnp.float32) * inv_own
    cot_whole = lax.psum(cot_input.astype(jnp.bfloat16), "head").astype(jnp.float32)
    row_dot = jnp.sum(cot_whole * gain_float[None, :] * input_hat, axis=-1, keepdims=True)
    cot_own = lax.dynamic_slice_in_dim(cot_whole, row_start, rows_own, 0)
    row_own = lax.dynamic_slice_in_dim(row_dot, row_start, rows_own, 0)
    input_grad = cotangent.astype(jnp.float32) + inv_own * (
        cot_own * gain_float[None, :] - own_hat * row_own / model_width
    )
    grad_gain = jnp.sum(cot_own * own_hat, axis=0)
    grad_zx, grad_dt, grad_bc, grad_out = (
        lax.psum_scatter(
            grad_zx.astype(jnp.bfloat16), "dp", scatter_dimension=0, tiled=True
        ).astype(jnp.float32),
        lax.psum_scatter(
            grad_dt.astype(jnp.bfloat16), "dp", scatter_dimension=0, tiled=True
        ).astype(jnp.float32),
        lax.psum_scatter(
            grad_bc.astype(jnp.bfloat16), "dp", scatter_dimension=0, tiled=True
        ).astype(jnp.float32),
        lax.psum_scatter(
            grad_out.astype(jnp.bfloat16), "dp", scatter_dimension=0, tiled=True
        ).astype(jnp.float32),
    )
    grad_chan = jnp.concatenate([slot_grads[0], grad_gate[None, :]], axis=0)
    grad_gain, grad_chan, grad_head, grad_convbc = lax.psum(
        (grad_gain, grad_chan, slot_grads[2], slot_grads[1]), "dp"
    )
    grad_bc, grad_convbc, grad_gain = (
        lax.psum(grad_bc.astype(jnp.bfloat16), "head").astype(jnp.float32),
        lax.psum(grad_convbc.astype(jnp.bfloat16), "head").astype(jnp.float32),
        lax.psum(grad_gain.astype(jnp.bfloat16), "head").astype(jnp.float32),
    )
    gain_next, gain_state = adam_update(norm_gain, gain_moments, grad_gain, rate_vector, 0.0)
    zx_next, zx_state = adam_update(proj_zx, zx_moments, grad_zx, rate_matrix, weight_decay)
    dt_next, dt_state = adam_update(proj_dt, dt_moments, grad_dt, rate_matrix, weight_decay)
    bc_next, bc_state = adam_update(proj_bc, bc_moments, grad_bc, rate_matrix, weight_decay)
    chan_next, chan_state = adam_update(chan_params, chan_moments, grad_chan, rate_vector, 0.0)
    convbc_next, convbc_state = adam_update(conv_bc, convbc_moments, grad_convbc, rate_vector, 0.0)
    head_next, head_state = adam_update(head_params, head_moments, grad_head, rate_vector, 0.0)
    outproj_next, outproj_state = adam_update(
        out_proj, out_moments, grad_out, rate_matrix, weight_decay
    )
    return (
        block_output,
        input_grad,
        gain_next,
        gain_state,
        zx_next,
        zx_state,
        dt_next,
        dt_state,
        bc_next,
        bc_state,
        chan_next,
        chan_state,
        convbc_next,
        convbc_state,
        head_next,
        head_state,
        outproj_next,
        outproj_state,
    )


def solution(mesh):
    placed = (
        P(("dp", "head"), None),
        P("dp"),
        P(("dp", "head"), None),
        P(),
        P("dp", None, "head"),
        P("dp", "head"),
        P("dp", None),
        P(None, "head"),
        P(),
        P(None, "head"),
        P(("head", "dp"), None),
        P(),
        P(None, "dp", None, "head"),
        P(None, "dp", "head"),
        P(None, "dp", None),
        P(None, None, "head"),
        P(),
        P(None, None, "head"),
        P(None, ("head", "dp"), None),
    )
    return jax.shard_map(
        shards,
        mesh=mesh,
        in_specs=placed,
        out_specs=(
            P(("dp", "head"), None),
            P(("dp", "head"), None),
            P(),
            P(),
            P("dp", None, "head"),
            P(None, "dp", None, "head"),
            P("dp", "head"),
            P(None, "dp", "head"),
            P("dp", None),
            P(None, "dp", None),
            P(None, "head"),
            P(None, None, "head"),
            P(),
            P(),
            P(None, "head"),
            P(None, None, "head"),
            P(("head", "dp"), None),
            P(None, ("head", "dp"), None),
        ),
        check_vma=False,
    )
```

profile of v0, /device:TPU:0, one launch (start us, length us, event | category | flops | bytes accessed | tf_op | source)
XLA Modules:
  0.0 714.8 jit_solution(882251160323522166)
XLA Ops:
  12.2 12.9 %all_gather.20 = bf16[1536,256]{1,0:T(8,128)(2,1)} all-gather(bf16[192,256]{1,0:T(8,128)(2,1)S(1)} %convert_element_type.153), channel_id=1, replica_groups=mesh['dp'=8,'head'=4] {'dp'}, dimensions={0}, use_global_device_ids=true | all-gather | bytes 884736 | tf_op jit(solution)/shard_map/all_gather | solution.py:102
  25.1 9.1 %all-gather = bf16[8,192,12]{1,2,0:T(8,128)(2,1)S(1)} all-gather(bf16[1,192,12]{1,2,0:T(8,128)(2,1)S(1)} %convert_bitcast_fusion), channel_id=1, replica_groups=mesh['dp'=8,'head'=4] {'dp'}, dimensions={0}, use_global_device_ids=true | all-gather | bytes 41472 | tf_op jit(solution)/shard_map/all_gather | solution.py:101
  35.1 40.8 %all-gather.6.cloned.1.call-done = bf16[1024,1536]{1,0:T(8,128)(2,1)} async-done(((bf16[256,1536]{1,0:T(8,128)(2,1)}), bf16[1024,1536]{1,0:T(8,128)(2,1)}) %all-gather.6.cloned.1.call-update) | async-done | bytes 3145744 | tf_op jit(solution)/shard_map/all_gather | solution.py:109
  82.8 33.0 %all-gather.8.cloned.1.call-done = bf16[1536,2,768]{2,1,0:T(2,128)(2,1)} async-done(((bf16[192,2,768]{2,1,0:T(2,128)(2,1)}), bf16[1536,2,768]{2,1,0:T(2,128)(2,1)}) %all-gather.8.cloned.1.call-update) | async-done | bytes 4718608 | tf_op jit(solution)/shard_map/all_gather | solution.py:100
  115.8 11.4 %reshape.322 = bf16[1536,1536,1]{1,0,2:T(8,128)(2,1)} reshape(bf16[1536,2,768]{2,1,0:T(2,128)(2,1)} %all-gather.8.cloned.1.call-done) | data formatting | bytes 9437184 | tf_op jit(solution)/shard_map/reshape | solution.py:105
  127.2 9.4 %fusion.160 = f32[4,256,1536]{1,2,0:T(8,128)} fusion(bf16[4,256,1536]{2,1,0:T(8,128)(2,1)S(1)} %bitcast.438, bf16[1536,1536,1]{1,0,2:T(8,128)(2,1)} %reshape.322), kind=kOutput, calls=%fused_computation.316 | convolution fusion | flops 4831838208 | bytes 14155776 | tf_op jit(solution)/shard_map/dot_general | solution.py:115
  136.6 39.3 %while.36 = (s32[]{:T(128)}, f32[4,256,768]{1,2,0:T(8,128)}, f32[5,768]{1,0:T(8,128)S(1)}, f32[4,256,1536]{1,2,0:T(8,128)}, f32[5,256]{1,0:T(8,128)S(1)}, /*inde...) while((s32[]{:T(128)}, f32[4,256,768]{1,2,0:T(8,128)}, ...), condition=%wide.region_2.3_spmd, body=%wide.region_1.2_spmd.sunk | while | flops 721925120 | bytes 12330901 | solution.py:129
  141.7 3.7 fusion.237
  151.5 3.7 fusion.237
  161.3 3.7 fusion.237
  171.1 3.7 fusion.237
  175.8 3.8 copy.117
  179.9 12.4 %psum.70 = f32[1024]{0:T(1024)S(1)} all-reduce(f32[1024]{0:T(1024)S(1)} %bitcast.479), channel_id=1, replica_groups=mesh['dp'=8,'head'=4] {'head'}, use_global_device_ids=true, to_apply=%region_4.5 | all-reduce | flops 1024 | bytes 8192 | tf_op jit(solution)/shard_map/psum | solution.py:132
  192.3 20.0 %all-gather.12.cloned.1.call-done = bf16[1024,1536]{1,0:T(8,128)(2,1)} async-done(((bf16[256,1536]{1,0:T(8,128)(2,1)}), bf16[1024,1536]{1,0:T(8,128)(2,1)}) %all-gather.12.cloned.1.call-update) | async-done | bytes 3145744 | tf_op jit(solution)/shard_map/all_gather | solution.py:142
  212.3 8.8 %fusion.111 = (f32[768]{0:T(1024)}, f32[1024]{0:T(1024)S(1)}, f32[1024,768]{1,0:T(8,128)}) fusion(f32[4,256,768]{2,1,0:T(8,128)} %copy.117, f32[1024]{0:T(1024)S(1)} %get-tuple-element.747, f32[768]{0:T(1024)S(1)} %slice_reduce_fusion.11, bf16[768,1536]{1,0:T(8,128)(2,1)} %all-gather.10.cloned.1.call-done, ...), kind=kOutput, calls=%fused_computation.196 | convolution fusion | flops 2425354496 | bytes 11814912 | tf_op jit(solution)/shard_map/dot_general | solution.py:144
  221.1 9.0 %psum.71 = f32[1024]{0:T(1024)S(1)} all-reduce(f32[1024]{0:T(1024)S(1)} %get-tuple-element.611), channel_id=1, replica_groups=mesh['dp'=8,'head'=4] {'head'}, use_global_device_ids=true, to_apply=%region_7.8 | all-reduce | flops 1024 | bytes 8192 | tf_op jit(solution)/shard_map/psum | solution.py:148
  230.1 4.2 fusion.108
  234.3 98.4 %while.37 = (s32[]{:T(128)}, f32[5,768]{1,0:T(8,128)S(1)}, f32[5,256]{1,0:T(8,128)S(1)}, f32[3,12]{1,0:T(4,128)S(1)}, bf16[4,256,1536]{2,1,0:T(8,128)(2,1)}, /*i...) while((s32[]{:T(128)}, f32[5,768]{1,0:T(8,128)S(1)}, ...), condition=%wide.region_27.28_spmd.clone, body=%wide.region_8.27_spmd.clone.sunk | while | flops 2164275456 | bytes 51899236 | solution.py:168
  239.9 2.8 fusion.257
  244.5 4.8 fusion.259
  250.7 3.7 fusion.258
  264.4 2.8 fusion.257
  269.0 4.8 fusion.259
  275.2 3.7 fusion.258
  288.9 2.8 fusion.257
  293.4 4.8 fusion.259
  299.7 3.7 fusion.258
  313.3 2.8 fusion.257
  317.9 4.8 fusion.259
  324.1 3.7 fusion.258
  332.8 4.0 convolution_convert_fusion.3
  338.6 6.6 convolution_convert_fusion.2
  345.2 3.4 copy.169
  350.5 5.1 fusion.163
  358.3 12.6 %reduce-scatter.12.cloned.1.call-done = bf16[192,256]{1,0:T(8,128)(2,1)} async-done(((bf16[1536,256]{1,0:T(8,128)(2,1)}), bf16[192,256]{1,0:T(8,128)(2,1)}) %reduce-scatter.12.cloned.1.call-update) | async-done | bytes 98320 | tf_op jit(solution)/shard_map/reduce_scatter | solution.py:201
  371.0 6.4 convolution_convert_fusion.1
  377.5 4.9 copy.144
  382.3 8.8 %convolution_convert_fusion = bf16[1536,2,768]{2,0,1:T(8,128)(2,1)} fusion(bf16[2,768,1024]{2,1,0:T(8,128)(2,1)} %bitcast.448, bf16[1024,1536]{1,0:T(8,128)(2,1)S(1)} %copy-done.1), kind=kOutput, calls=%fused_computation.181 | convolution fusion | flops 4834197504 | bytes 11010048 | tf_op jit(solution)/shard_map/dot_general | solution.py:179
  399.3 9.0 %reduce-scatter.16.cloned.1.call-done = bf16[192,12]{1,0:T(8,128)(2,1)} async-done(((bf16[1536,12]{1,0:T(8,128)(2,1)}), bf16[192,12]{1,0:T(8,128)(2,1)}) %reduce-scatter.16.cloned.1.call-update) | async-done | bytes 4624
  410.5 44.1 %reduce-scatter.14.cloned.1.call-done = bf16[96,1536]{1,0:T(8,128)(2,1)} async-done(((bf16[768,1536]{1,0:T(8,128)(2,1)}), bf16[96,1536]{1,0:T(8,128)(2,1)}) %reduce-scatter.14.cloned.1.call-update) | async-done | bytes 294928 | tf_op jit(solution)/shard_map/reduce_scatter | solution.py:204
  458.5 122.8 %all-reduce.34.cloned.1.call-done = (bf16[1024,1536]{1,0:T(8,128)(2,1)}, bf16[192,256]{1,0:T(8,128)(2,1)}) async-done(((bf16[1024,1536]{1,0:T(8,128)(2,1)}, bf16[192,256]{1,0:T(8,128)(2,1)}), (bf16[1024,1536]{1,0:T(8,128)(2,1)}, bf16[192,256]{1,0:T(8,128)(2,1)})) %all-reduce.34.cloned.1.call-update) | async-done | bytes 3244048 | tf_op jit(solution)/shard_map/psum | solution.py:186
  581.3 5.6 convert_element_type.172
  590.6 52.5 %reduce-scatter.8.cloned.1.call-done = bf16[256,1536]{1,0:T(8,128)(2,1)} async-done(((bf16[1024,1536]{1,0:T(8,128)(2,1)}), bf16[256,1536]{1,0:T(8,128)(2,1)}) %reduce-scatter.8.cloned.1.call-update) | async-done | bytes 786448 | tf_op jit(solution)/shard_map/reduce_scatter | solution.py:135
  643.1 4.9 fusion.118
  648.0 25.3 %all-reduce.29 = (bf16[1536]{0:T(1024)(128)(2,1)}, f32[6,768]{1,0:T(8,128)}, bf16[5,256]{1,0:T(8,128)(2,1)}, f32[3,12]{1,0:T(4,128)}) all-reduce(f32[1536]{0:T(1024)} %get-tuple-element.712, f32[6,768]{1,0:T(8,128)} %pad_maximum_fusion.5, f32[5,256]{1,0:T(8,128)S(1)} %get-tuple-element.358, ...), channel_id=1, replica_groups=mesh['dp'=8,'head'=4] {'dp'}, use_global_device_ids=true, to_apply=%region_31.32 | all-reduce | flops 7460 | bytes 54048 | tf_op jit(solution)/shard_map/psum | solution.py:209
  675.2 11.6 %all-reduce.30 = (bf16[1536]{0:T(1024)(128)(2,1)S(1)}, bf16[5,256]{1,0:T(8,128)(2,1)S(1)}) all-reduce(bf16[1536]{0:T(1024)(128)(2,1)} %get-tuple-element.664, bf16[5,256]{1,0:T(8,128)(2,1)} %get-tuple-element.666), channel_id=1, replica_groups=mesh['dp'=8,'head'=4] {'head'}, use_global_device_ids=true, to_apply=%region_32.33 | all-reduce | flops 2816 | bytes 11264 | tf_op jit(solution)/shard_map/psum | solution.py:215
  692.8 7.3 %reduce-scatter.10.cloned.1.call-done = bf16[192,2,768]{2,0,1:T(8,128)(2,1)} async-done(((bf16[1536,2,768]{2,0,1:T(8,128)(2,1)}), bf16[192,2,768]{2,0,1:T(8,128)(2,1)}) %reduce-scatter.10.cloned.1.call-update) | async-done | bytes 589840 | tf_op jit(solution)/shard_map/reduce_scatter | solution.py:195
  702.5 3.2 copy.136
  (400 shorter events, 125.4 us)
Async XLA Ops:
  7.2 3.4 copy-start.11
  7.2 4.9 copy-start.35
  7.2 4.9 copy-start.17
  7.2 17.9 %copy-start.30 = (f32[192,12]{0,1:T(8,128)S(1)}, f32[192,12]{0,1:T(8,128)}, u32[]{:S(2)}) copy-start(f32[192,12]{0,1:T(8,128)} %param.28) | copy-start | bytes 27652
  7.2 27.1 %copy-start.27 = (f32[3,12]{1,0:T(4,128)S(1)}, f32[3,12]{1,0:T(4,128)}, u32[]{:S(2)}) copy-start(f32[3,12]{1,0:T(4,128)} %param.32) | copy-start | bytes 436
  7.2 27.1 %copy-start.42 = (s32[4]{0:T(128)S(1)}, s32[4]{0:T(128)}, u32[]{:S(2)}) copy-start(s32[4]{0:T(128)} %param.24) | copy-start | bytes 52
  7.3 27.8 %copy-start.13 = (f32[6,768]{1,0:T(8,128)S(1)}, f32[6,768]{1,0:T(8,128)}, u32[]{:S(2)}) copy-start(f32[6,768]{1,0:T(8,128)} %param.30) | copy-start | bytes 55300
  7.3 68.6 %all-gather.6.cloned.1.call-start = ((), (), s32[]{:S(2)}) async-start(), calls=%async_computation.5 | async-start | bytes 3932160 | tf_op jit(solution)/shard_map/all_gather | solution.py:109
  8.0 107.8 %all-gather.8.cloned.1.call-start = ((), (), s32[]{:S(2)}) async-start(), calls=%async_computation.6 | async-start | bytes 5308416 | tf_op jit(solution)/shard_map/all_gather | solution.py:100
  10.6 181.7 %all-gather.10.cloned.1.call-start = ((), (), s32[]{:S(2)}) async-start(), calls=%async_computation.7 | async-start | bytes 2654208 | tf_op jit(solution)/shard_map/all_gather | solution.py:103
  11.4 200.9 %all-gather.12.cloned.1.call-start = ((), (), s32[]{:S(2)}) async-start(), calls=%async_computation.9 | async-start | bytes 3932160 | tf_op jit(solution)/shard_map/all_gather | solution.py:142
  12.0 358.9 %reduce-scatter.12.cloned.1.call-start = ((), (), s32[]{:S(2)}) async-start(), calls=%async_computation.11 | async-start | bytes 884736 | tf_op jit(solution)/shard_map/reduce_scatter | solution.py:201
  12.1 67.4 %copy-start.24 = (f32[1536]{0:T(1024)}, f32[1536]{0:T(1024)S(1)}, u32[]{:S(2)}) copy-start(f32[1536]{0:T(1024)S(1)} %convert_element_type.150) | copy-start | bytes 18436
  75.8 2.8 copy-start.2
  79.8 47.4 %copy-start = (bf16[1024,1536]{1,0:T(8,128)(2,1)}, bf16[1024,1536]{1,0:T(8,128)(2,1)S(1)}, u32[]{:S(2)}) copy-start(bf16[1024,1536]{1,0:T(8,128)(2,1)S(1)} %fusion.100) | copy-start | bytes 9437188
  127.2 9.4 %copy-start.22 = (f32[5,256]{1,0:T(8,128)S(1)}, f32[5,256]{1,0:T(8,128)}, u32[]{:S(2)}) copy-start(f32[5,256]{1,0:T(8,128)} %param.31) | copy-start | bytes 15364
  175.8 3.8 copy-start.4
  212.3 17.8 %copy-start.6 = (f32[4,256,768]{2,1,0:T(8,128)S(1)}, f32[4,256,768]{2,1,0:T(8,128)}, u32[]{:S(2)}) copy-start(f32[4,256,768]{2,1,0:T(8,128)} %copy.117) | copy-start | bytes 9437188
  250.7 5.6 copy-start.20
  275.2 5.6 copy-start.20
  299.6 5.6 copy-start.20
  324.1 5.6 copy-start.20
  332.7 4.1 copy-start.14
  332.8 4.1 copy-start.15
  332.8 4.1 copy-start.28
  332.8 4.1 copy-start.29
  332.8 4.2 copy-start.1
  336.9 71.4 %reduce-scatter.16.cloned.1.call-start = ((), (), s32[]{:S(2)}) async-start(), calls=%async_computation.13 | async-start | bytes 442368
  338.5 116.1 %reduce-scatter.14.cloned.1.call-start = ((), (), s32[]{:S(2)}) async-start(), calls=%async_computation.12 | async-start | bytes 2654208 | tf_op jit(solution)/shard_map/reduce_scatter | solution.py:204
  345.2 236.1 %all-reduce.34.cloned.1.call-start = ((), (), s32[]{:S(2)}) async-start(), calls=%async_computation.14 | async-start | bytes 6488064 | tf_op jit(solution)/shard_map/psum | solution.py:186
  350.5 5.1 copy-start.9
  350.5 5.1 copy-start.21
  370.9 272.2 %reduce-scatter.8.cloned.1.call-start = ((), (), s32[]{:S(2)}) async-start(), calls=%async_computation.8 | async-start | bytes 3932160 | tf_op jit(solution)/shard_map/reduce_scatter | solution.py:135
  377.4 322.7 %reduce-scatter.10.cloned.1.call-start = ((), (), s32[]{:S(2)}) async-start(), calls=%async_computation.10 | async-start | bytes 5308416 | tf_op jit(solution)/shard_map/reduce_scatter | solution.py:195
  391.1 2.5 copy-start.39
  391.1 3.1 copy-start.36
  391.1 3.1 copy-start.34
  391.2 7.5 %copy-start.40 = (f32[768]{0:T(1024)S(1)}, f32[768]{0:T(1024)}, u32[]{:S(2)}) copy-start(f32[768]{0:T(1024)} %get-tuple-element.610) | copy-start | bytes 9220
  391.2 7.5 %copy-start.16 = (f32[5,768]{1,0:T(8,128)S(1)}, f32[5,768]{1,0:T(8,128)}, u32[]{:S(2)}) copy-start(f32[5,768]{1,0:T(8,128)} %copy-done.15) | copy-start | bytes 46084
  391.2 18.0 %copy-start.31 = (f32[192,12]{0,1:T(8,128)S(1)}, f32[192,12]{0,1:T(8,128)}, u32[]{:S(2)}) copy-start(f32[192,12]{0,1:T(8,128)} %param.28) | copy-start | bytes 27652
  391.2 63.4 %copy-start.12 = (f32[96,1536]{1,0:T(8,128)S(1)}, f32[96,1536]{1,0:T(8,128)}, u32[]{:S(2)}) copy-start(f32[96,1536]{1,0:T(8,128)} %param.33) | copy-start | bytes 1769476
  581.3 5.6 copy-start.3
  581.3 5.6 copy-start.5
  581.3 5.6 copy-start.25
  581.3 5.6 copy-start.33
  586.9 2.0 copy-start.18
  586.9 2.0 copy-start.23
  643.1 57.0 %copy-start.7 = (f32[192,2,768]{2,1,0:T(2,128)S(1)}, f32[192,2,768]{2,1,0:T(2,128)}, u32[]{:S(2)}) copy-start(f32[192,2,768]{2,1,0:T(2,128)} %param.27) | copy-start | bytes 3538948
  (11 other events, 15.0 us)
Sparse Core Ops, SparseCore 0:
  9.6 66.1 all-gather.5
  78.3 37.4 all-gather.7
  118.2 28.8 all-gather.9
  148.6 63.6 all-gather.11
  337.0 33.8 reduce-scatter.11
  374.4 33.8 reduce-scatter.15
  412.2 42.3 reduce-scatter.13
  457.0 124.2 all-reduce.33
  583.6 59.4 reduce-scatter.7
  646.4 53.6 reduce-scatter.9
where the time goes:
time: 721 us; the launch traced here: 715 us
  waiting for transfers between devices  343 us (48%)
  matrix products  125 us (17%)
  blocking collectives  80.3 us (11%)
  other arithmetic  75.3 us (10%)
  local copies, waits for them, and re-layouts  73.4 us (10%)
  between operations  15 us (2%)
    psum x1, waiting for transfers between devices, shards(): lax.psum(cot_input.astype(jnp.bfloat16), 'head').astype(jnp.float32)  123 us
    dot_general x16, matrix products, mixer_slot(): output = jnp.einsum('hts,shp->thp', weights, head_values, precision=highest)  59.5 us
    reduce_scatter x1, waiting for transfers between devices, shards(): lax.psum_scatter(jnp.dot(normed_out, out_full, preferred_element_type=jnp...  52.5 us
    reduce_scatter x1, waiting for transfers between devices, shards(): lax.psum_scatter(grad_out.astype(jnp.bfloat16), 'dp', scatter_dimension=0...  44.1 us
    all_gather x1, waiting for transfers between devices, shards(): input_all = lax.all_gather(block_input, 'head', axis=0, tiled=True)  40.8 us
    all_gather x1, waiting for transfers between devices, shards(): lax.all_gather(proj_zx.astype(jnp.bfloat16), 'dp', axis=0, tiled=True)  33 us
    psum x1, blocking collectives, shards(): lax.psum((grad_gain, grad_chan, slot_grads[2], slot_grads[1]), 'dp')  25.3 us
    squeeze x16, local copies, waits for them, and re-layouts, shards(): lax.map(forward_slot, (proj_slots, bc_slots, step_slots))  20.2 us
  transfers between devices with their start and end apart: 10, of which 9 were waited for; matrix products, arithmetic and copies ran while one was open for 21% of the time, Pallas kernels for 0%

commit v1 on v0

--- a/solution.py
+++ b/solution.py
@@ -183,7 +183,9 @@
     grad_bc = jnp.dot(normed_in.T, cot_bc, preferred_element_type=jnp.float32)
     inv_own = lax.dynamic_slice_in_dim(inv_norm, row_start, rows_own, 0)
     own_hat = block_input.astype(jnp.float32) * inv_own
-    cot_whole = lax.psum(cot_input.astype(jnp.bfloat16), "head").astype(jnp.float32)
+    cot_whole = jnp.sum(lax.all_gather(cot_input.astype(jnp.bfloat16), "head"), axis=0).astype(
+        jnp.float32
+    )
     row_dot = jnp.sum(cot_whole * gain_float[None, :] * input_hat, axis=-1, keepdims=True)
     cot_own = lax.dynamic_slice_in_dim(cot_whole, row_start, rows_own, 0)
     row_own = lax.dynamic_slice_in_dim(row_dot, row_start, rows_own, 0)

time: 721 us -> 886 us (1.23)
  waiting for transfers between devices: 343 us -> 507 us
    all_gather x0 -> x1, waiting for transfers between devices: none -> 212 us  [shards(): lax.all_gather(cot_input.astype(jnp.bfloat16), 'head')]
    psum x1, waiting for transfers between devices: 123 us -> 23.4 us  [shards(): lax.psum(grad_bc.astype(jnp.bfloat16), 'head').astype(jnp.float32)]
    reduce_scatter x1, waiting for transfers between devices: 7.3 us -> 53.2 us  [shards(): lax.psum_scatter(grad_zx.astype(jnp.bfloat16), 'dp', scatter_dimension=0,...]
    reduce_scatter x1, waiting for transfers between devices: 12.6 us -> 32.3 us  [shards(): lax.psum_scatter(grad_bc.astype(jnp.bfloat16), 'dp', scatter_dimension=0,...]
    unnamed x11 -> x12, waiting for transfers between devices: 10.4 us -> 1.35 us
  transfers between devices with their start and end apart: 10 -> 11, of which waited for: 9 -> 9; matrix products, arithmetic and copies ran while one was open for 21% -> 17% of each run, Pallas kernels for 0% -> 0%
where the time goes in v1:
time: 886 us; the launch traced here: 880 us
  waiting for transfers between devices  507 us (57%)
  matrix products  124 us (14%)
  other arithmetic  79.4 us (9%)
  blocking collectives  78.6 us (9%)
  local copies, waits for them, and re-layouts  73.9 us (8%)
  between operations  14.9 us (2%)
    all_gather x1, waiting for transfers between devices, shards(): lax.all_gather(cot_input.astype(jnp.bfloat16), 'head')  212 us
    dot_general x16, matrix products, mixer_slot(): output = jnp.einsum('hts,shp->thp', weights, head_values, precision=highest)  59.5 us
    reduce_scatter x1, waiting for transfers between devices, shards(): lax.psum_scatter(grad_zx.astype(jnp.bfloat16), 'dp', scatter_dimension=0,...  53.2 us
    reduce_scatter x1, waiting for transfers between devices, shards(): lax.psum_scatter(jnp.dot(normed_out, out_full, preferred_element_type=jnp...  47.2 us
    reduce_scatter x1, waiting for transfers between devices, shards(): lax.psum_scatter(grad_out.astype(jnp.bfloat16), 'dp', scatter_dimension=0...  43.5 us
    all_gather x1, waiting for transfers between devices, shards(): input_all = lax.all_gather(block_input, 'head', axis=0, tiled=True)  40.7 us
    all_gather x1, waiting for transfers between devices, shards(): lax.all_gather(proj_zx.astype(jnp.bfloat16), 'dp', axis=0, tiled=True)  33 us
    reduce_scatter x1, waiting for transfers between devices, shards(): lax.psum_scatter(grad_bc.astype(jnp.bfloat16), 'dp', scatter_dimension=0,...  32.3 us
  transfers between devices with their start and end apart: 11, of which 9 were waited for; matrix products, arithmetic and copies ran while one was open for 17% of the time, Pallas kernels for 0%

profile of v1, /device:TPU:0, one launch (start us, length us, event | category | flops | bytes accessed | tf_op | source)
XLA Modules:
  0.0 880.1 jit_solution(1575022422675598000)
XLA Ops:
  12.2 12.9 %all_gather.26 = bf16[1536,256]{1,0:T(8,128)(2,1)} all-gather(bf16[192,256]{1,0:T(8,128)(2,1)S(1)} %convert_element_type.155), channel_id=1, replica_groups=mesh['dp'=8,'head'=4] {'dp'}, dimensions={0}, use_global_device_ids=true | all-gather | bytes 884736 | tf_op jit(solution)/shard_map/all_gather | solution.py:102
  25.1 9.1 %all-gather.1 = bf16[8,192,12]{1,2,0:T(8,128)(2,1)S(1)} all-gather(bf16[1,192,12]{1,2,0:T(8,128)(2,1)S(1)} %convert_bitcast_fusion), channel_id=1, replica_groups=mesh['dp'=8,'head'=4] {'dp'}, dimensions={0}, use_global_device_ids=true | all-gather | bytes 41472 | tf_op jit(solution)/shard_map/all_gather | solution.py:101
  35.1 40.7 %all-gather.8.cloned.1.call-done = bf16[1024,1536]{1,0:T(8,128)(2,1)} async-done(((bf16[256,1536]{1,0:T(8,128)(2,1)}), bf16[1024,1536]{1,0:T(8,128)(2,1)}) %all-gather.8.cloned.1.call-update) | async-done | bytes 3145744 | tf_op jit(solution)/shard_map/all_gather | solution.py:109
  82.8 33.0 %all-gather.10.cloned.1.call-done = bf16[1536,2,768]{2,1,0:T(2,128)(2,1)} async-done(((bf16[192,2,768]{2,1,0:T(2,128)(2,1)}), bf16[1536,2,768]{2,1,0:T(2,128)(2,1)}) %all-gather.10.cloned.1.call-update) | async-done | bytes 4718608 | tf_op jit(solution)/shard_map/all_gather | solution.py:100
  115.8 11.4 %reshape.323 = bf16[1536,1536,1]{1,0,2:T(8,128)(2,1)} reshape(bf16[1536,2,768]{2,1,0:T(2,128)(2,1)} %all-gather.10.cloned.1.call-done) | data formatting | bytes 9437184 | tf_op jit(solution)/shard_map/reshape | solution.py:105
  127.2 9.4 %fusion.160 = f32[4,256,1536]{1,2,0:T(8,128)} fusion(bf16[4,256,1536]{2,1,0:T(8,128)(2,1)S(1)} %bitcast.439, bf16[1536,1536,1]{1,0,2:T(8,128)(2,1)} %reshape.323), kind=kOutput, calls=%fused_computation.316 | convolution fusion | flops 4831838208 | bytes 14155776 | tf_op jit(solution)/shard_map/dot_general | solution.py:115
  136.6 39.2 %while.36 = (s32[]{:T(128)}, f32[4,256,768]{1,2,0:T(8,128)}, f32[5,768]{1,0:T(8,128)S(1)}, f32[4,256,1536]{1,2,0:T(8,128)}, f32[5,256]{1,0:T(8,128)S(1)}, /*inde...) while((s32[]{:T(128)}, f32[4,256,768]{1,2,0:T(8,128)}, ...), condition=%wide.region_2.3_spmd, body=%wide.region_1.2_spmd.sunk | while | flops 721925120 | bytes 12330901 | solution.py:129
  141.7 3.7 fusion.237
  151.5 3.7 fusion.237
  161.3 3.7 fusion.237
  171.0 3.7 fusion.237
  175.8 3.8 copy.117
  179.8 12.4 %psum.63 = f32[1024]{0:T(1024)S(1)} all-reduce(f32[1024]{0:T(1024)S(1)} %bitcast.481), channel_id=1, replica_groups=mesh['dp'=8,'head'=4] {'head'}, use_global_device_ids=true, to_apply=%region_4.5 | all-reduce | flops 1024 | bytes 8192 | tf_op jit(solution)/shard_map/psum | solution.py:132
  192.3 20.0 %all-gather.14.cloned.1.call-done = bf16[1024,1536]{1,0:T(8,128)(2,1)} async-done(((bf16[256,1536]{1,0:T(8,128)(2,1)}), bf16[1024,1536]{1,0:T(8,128)(2,1)}) %all-gather.14.cloned.1.call-update) | async-done | bytes 3145744 | tf_op jit(solution)/shard_map/all_gather | solution.py:142
  212.3 8.7 fusion.111
  221.0 9.0 %psum.64 = f32[1024]{0:T(1024)S(1)} all-reduce(f32[1024]{0:T(1024)S(1)} %get-tuple-element.611), channel_id=1, replica_groups=mesh['dp'=8,'head'=4] {'head'}, use_global_device_ids=true, to_apply=%region_7.8 | all-reduce | flops 1024 | bytes 8192 | tf_op jit(solution)/shard_map/psum | solution.py:148
  230.0 4.2 fusion.108
  234.2 98.4 %while.37 = (s32[]{:T(128)}, f32[5,768]{1,0:T(8,128)S(1)}, f32[5,256]{1,0:T(8,128)S(1)}, f32[3,12]{1,0:T(4,128)S(1)}, bf16[4,256,1536]{2,1,0:T(8,128)(2,1)}, /*i...) while((s32[]{:T(128)}, f32[5,768]{1,0:T(8,128)S(1)}, ...), condition=%wide.region_27.28_spmd.clone, body=%wide.region_8.27_spmd.clone.sunk | while | flops 2164275456 | bytes 51899236 | solution.py:168
  244.4 4.8 fusion.259
  250.6 3.7 fusion.258
  268.8 4.8 fusion.259
  275.0 3.7 fusion.258
  288.7 2.8 fusion.257
  293.3 4.8 fusion.259
  299.5 3.7 fusion.258
  313.2 2.8 fusion.257
  317.7 4.8 fusion.259
  324.0 3.7 fusion.258
  332.7 4.1 convolution_convert_fusion.3
  338.4 32.3 %reduce-scatter.12.cloned.1.call-done = bf16[192,256]{1,0:T(8,128)(2,1)} async-done(((bf16[1536,256]{1,0:T(8,128)(2,1)}), bf16[192,256]{1,0:T(8,128)(2,1)}) %reduce-scatter.12.cloned.1.call-update) | async-done | bytes 98320 | tf_op jit(solution)/shard_map/reduce_scatter | solution.py:203
  370.8 6.6 convolution_convert_fusion.2
  377.5 4.7 copy.144
  382.1 8.7 convolution_convert_fusion
  391.0 3.3 copy.169
  396.2 5.1 fusion.163
  405.4 5.8 convolution_convert_fusion.1
  421.6 23.4 %all-reduce.33.cloned.1.call-done = bf16[192,256]{1,0:T(8,128)(2,1)} async-done(((bf16[192,256]{1,0:T(8,128)(2,1)}), bf16[192,256]{1,0:T(8,128)(2,1)}) %all-reduce.33.cloned.1.call-update) | async-done | bytes 98320 | tf_op jit(solution)/shard_map/psum | solution.py:215
  447.6 43.5 %reduce-scatter.14.cloned.1.call-done = bf16[96,1536]{1,0:T(8,128)(2,1)} async-done(((bf16[768,1536]{1,0:T(8,128)(2,1)}), bf16[96,1536]{1,0:T(8,128)(2,1)}) %reduce-scatter.14.cloned.1.call-update) | async-done | bytes 294928 | tf_op jit(solution)/shard_map/reduce_scatter | solution.py:206
  491.0 2.9 fusion.127
  495.1 53.2 %reduce-scatter.10.cloned.1.call-done = bf16[192,2,768]{2,0,1:T(8,128)(2,1)} async-done(((bf16[1536,2,768]{2,0,1:T(8,128)(2,1)}), bf16[192,2,768]{2,0,1:T(8,128)(2,1)}) %reduce-scatter.10.cloned.1.call-update) | async-done | bytes 589840 | tf_op jit(solution)/shard_map/reduce_scatter | solution.py:197
  550.7 3.2 copy.136
  555.8 212.0 %all-gather.16.cloned.1.call-done = bf16[4096,1536]{1,0:T(8,128)(2,1)} async-done(((bf16[1024,1536]{1,0:T(8,128)(2,1)}), bf16[4096,1536]{1,0:T(8,128)(2,1)}) %all-gather.16.cloned.1.call-update) | async-done | bytes 12582928 | tf_op jit(solution)/shard_map/all_gather | solution.py:186
  767.9 8.7 reduce_sum.368
  776.6 3.5 convert_element_type.174
  781.6 47.2 %reduce-scatter.8.cloned.1.call-done = bf16[256,1536]{1,0:T(8,128)(2,1)} async-done(((bf16[1024,1536]{1,0:T(8,128)(2,1)}), bf16[256,1536]{1,0:T(8,128)(2,1)}) %reduce-scatter.8.cloned.1.call-update) | async-done | bytes 786448 | tf_op jit(solution)/shard_map/reduce_scatter | solution.py:135
  828.9 4.3 fusion.118
  833.2 24.0 %all-reduce.29 = (bf16[1536]{0:T(1024)(128)(2,1)S(1)}, f32[6,768]{1,0:T(8,128)S(1)}, bf16[5,256]{1,0:T(8,128)(2,1)S(1)}, f32[3,12]{1,0:T(4,128)S(1)}) all-reduce(f32[1536]{0:T(1024)S(1)} %get-tuple-element.710, f32[6,768]{1,0:T(8,128)S(1)} %copy-done.28, ...), channel_id=1, replica_groups=mesh['dp'=8,'head'=4] {'dp'}, use_global_device_ids=true, to_apply=%region_31.32 | all-reduce | flops 7460 | bytes 54048 | tf_op jit(solution)/shard_map/psum | solution.py:211
  858.4 11.1 %all-reduce.30 = (bf16[1536]{0:T(1024)(128)(2,1)S(1)}, bf16[5,256]{1,0:T(8,128)(2,1)S(1)}) all-reduce(bf16[1536]{0:T(1024)(128)(2,1)S(1)} %get-tuple-element.664, bf16[5,256]{1,0:T(8,128)(2,1)S(1)} %get-tuple-element.666), channel_id=1, replica_groups=mesh['dp'=8,'head'=4] {'head'}, use_global_device_ids=true, to_apply=%region_32.33 | all-reduce | flops 2816 | bytes 11264 | tf_op jit(solution)/shard_map/psum | solution.py:217
  (434 shorter events, 127.1 us)
Async XLA Ops:
  7.2 4.9 copy-start.43
  7.2 4.9 copy-start.17
  7.2 17.9 %copy-start.36 = (f32[192,12]{0,1:T(8,128)S(1)}, f32[192,12]{0,1:T(8,128)}, u32[]{:S(2)}) copy-start(f32[192,12]{0,1:T(8,128)} %param.28) | copy-start | bytes 27652
  7.2 27.1 %copy-start.31 = (f32[3,12]{1,0:T(4,128)S(1)}, f32[3,12]{1,0:T(4,128)}, u32[]{:S(2)}) copy-start(f32[3,12]{1,0:T(4,128)} %param.32) | copy-start | bytes 436
  7.2 27.2 %copy-start.57 = (s32[4]{0:T(128)S(1)}, s32[4]{0:T(128)}, u32[]{:S(2)}) copy-start(s32[4]{0:T(128)} %param.24) | copy-start | bytes 52
  7.3 27.8 %copy-start.12 = (f32[6,768]{1,0:T(8,128)S(1)}, f32[6,768]{1,0:T(8,128)}, u32[]{:S(2)}) copy-start(f32[6,768]{1,0:T(8,128)} %param.30) | copy-start | bytes 55300
  7.3 68.6 %all-gather.8.cloned.1.call-start = ((), (), s32[]{:S(2)}) async-start(), calls=%async_computation.5 | async-start | bytes 3932160 | tf_op jit(solution)/shard_map/all_gather | solution.py:109
  8.0 107.8 %all-gather.10.cloned.1.call-start = ((), (), s32[]{:S(2)}) async-start(), calls=%async_computation.6 | async-start | bytes 5308416 | tf_op jit(solution)/shard_map/all_gather | solution.py:100
  10.6 181.7 %all-gather.12.cloned.1.call-start = ((), (), s32[]{:S(2)}) async-start(), calls=%async_computation.7 | async-start | bytes 2654208 | tf_op jit(solution)/shard_map/all_gather | solution.py:103
  11.4 200.9 %all-gather.14.cloned.1.call-start = ((), (), s32[]{:S(2)}) async-start(), calls=%async_computation.9 | async-start | bytes 3932160 | tf_op jit(solution)/shard_map/all_gather | solution.py:142
  12.0 358.8 %reduce-scatter.12.cloned.1.call-start = ((), (), s32[]{:S(2)}) async-start(), calls=%async_computation.11 | async-start | bytes 884736 | tf_op jit(solution)/shard_map/reduce_scatter | solution.py:203
  12.1 67.4 %copy-start.26 = (f32[1536]{0:T(1024)}, f32[1536]{0:T(1024)S(1)}, u32[]{:S(2)}) copy-start(f32[1536]{0:T(1024)S(1)} %convert_element_type.152) | copy-start | bytes 18436
  34.4 47.5 %copy-start.22 = (bf16[1536,12]{0,1:T(8,128)(2,1)}, bf16[1536,12]{0,1:T(8,128)(2,1)S(1)}, u32[]{:S(2)}) copy-start(bf16[1536,12]{0,1:T(8,128)(2,1)S(1)} %reshape.309) | copy-start | bytes 110596
  79.8 47.4 %copy-start = (bf16[1024,1536]{1,0:T(8,128)(2,1)}, bf16[1024,1536]{1,0:T(8,128)(2,1)S(1)}, u32[]{:S(2)}) copy-start(bf16[1024,1536]{1,0:T(8,128)(2,1)S(1)} %fusion.100) | copy-start | bytes 9437188
  127.2 9.4 %copy-start.24 = (f32[5,256]{1,0:T(8,128)S(1)}, f32[5,256]{1,0:T(8,128)}, u32[]{:S(2)}) copy-start(f32[5,256]{1,0:T(8,128)} %param.31) | copy-start | bytes 15364
  212.3 17.7 %copy-start.5 = (f32[4,256,768]{2,1,0:T(8,128)S(1)}, f32[4,256,768]{2,1,0:T(8,128)}, u32[]{:S(2)}) copy-start(f32[4,256,768]{2,1,0:T(8,128)} %copy.117) | copy-start | bytes 9437188
  250.6 5.6 copy-start.20
  275.0 5.6 copy-start.20
  299.5 5.6 copy-start.20
  323.9 5.6 copy-start.20
  336.8 82.7 %reduce-scatter.16.cloned.1.call-start = ((), (), s32[]{:S(2)}) async-start(), calls=%async_computation.15 | async-start | bytes 442368
  338.4 106.6 %all-reduce.33.cloned.1.call-start = ((), (), s32[]{:S(2)}) async-start(), calls=%async_computation.12 | async-start | bytes 196608 | tf_op jit(solution)/shard_map/psum | solution.py:215
  370.8 120.2 %reduce-scatter.14.cloned.1.call-start = ((), (), s32[]{:S(2)}) async-start(), calls=%async_computation.13 | async-start | bytes 2654208 | tf_op jit(solution)/shard_map/reduce_scatter | solution.py:206
  377.4 170.8 %reduce-scatter.10.cloned.1.call-start = ((), (), s32[]{:S(2)}) async-start(), calls=%async_computation.10 | async-start | bytes 5308416 | tf_op jit(solution)/shard_map/reduce_scatter | solution.py:197
  390.9 377.0 %all-gather.16.cloned.1.call-start = ((), (), s32[]{:S(2)}) async-start(), calls=%async_computation.14 | async-start | bytes 15728640 | tf_op jit(solution)/shard_map/all_gather | solution.py:186
  396.1 5.1 copy-start.8
  396.2 5.1 copy-start.21
  404.0 424.8 %reduce-scatter.8.cloned.1.call-start = ((), (), s32[]{:S(2)}) async-start(), calls=%async_computation.8 | async-start | bytes 3932160 | tf_op jit(solution)/shard_map/reduce_scatter | solution.py:135
  411.3 7.5 copy-start.55
  411.3 7.5 copy-start.16
  411.3 9.0 %copy-start.37 = (f32[192,12]{0,1:T(8,128)S(1)}, f32[192,12]{0,1:T(8,128)}, u32[]{:S(2)}) copy-start(f32[192,12]{0,1:T(8,128)} %param.28) | copy-start | bytes 27652
  411.4 33.6 %copy-start.18 = (f32[192,256]{1,0:T(8,128)S(1)}, f32[192,256]{1,0:T(8,128)}, u32[]{:S(2)}) copy-start(f32[192,256]{1,0:T(8,128)} %param.29) | copy-start | bytes 589828
  411.4 33.6 %copy-start.25 = (f32[2,192,256]{2,1,0:T(8,128)S(1)}, f32[2,192,256]{2,1,0:T(8,128)}, u32[]{:S(2)}) copy-start(f32[2,192,256]{2,1,0:T(8,128)} %param.37) | copy-start | bytes 1179652
  447.5 100.7 %copy-start.6 = (f32[192,2,768]{2,1,0:T(2,128)S(1)}, f32[192,2,768]{2,1,0:T(2,128)}, u32[]{:S(2)}) copy-start(f32[192,2,768]{2,1,0:T(2,128)} %param.27) | copy-start | bytes 3538948
  780.1 48.6 %copy-start.53 = (f32[256,1]{0,1:T(1,128)S(1)}, f32[256,1]{0,1:T(1,128)}, u32[]{:S(2)}) copy-start(f32[256,1]{0,1:T(1,128)} %constant_dynamic-slice_fusion.1) | copy-start | bytes 3076
  780.2 48.6 %copy-start.54 = (f32[256]{0:T(256)S(1)}, f32[256]{0:T(256)}, u32[]{:S(2)}) copy-start(f32[256]{0:T(256)} %dynamic-slice.6) | copy-start | bytes 3076
  828.8 4.4 copy-start.35
  828.8 28.4 %copy-start.33 = (f32[3,12]{1,0:T(4,128)S(1)}, f32[3,12]{1,0:T(4,128)}, u32[]{:S(2)}) copy-start(f32[3,12]{1,0:T(4,128)} %copy-done.32) | copy-start | bytes 436
  828.8 28.4 %copy-start.51 = (f32[1,3,12]{2,0,1:T(1,128)S(1)}, f32[1,3,12]{2,0,1:T(1,128)}, u32[]{:S(2)}) copy-start(f32[1,3,12]{2,0,1:T(1,128)} %get-tuple-element.749) | copy-start | bytes 436
  828.8 28.4 %copy-start.52 = (f32[1,3,12]{2,0,1:T(1,128)S(1)}, f32[1,3,12]{2,0,1:T(1,128)}, u32[]{:S(2)}) copy-start(f32[1,3,12]{2,0,1:T(1,128)} %get-tuple-element.750) | copy-start | bytes 436
  828.8 40.7 %copy-start.46 = (f32[1,5,256]{2,0,1:T(1,128)S(1)}, f32[1,5,256]{2,0,1:T(1,128)}, u32[]{:S(2)}) copy-start(f32[1,5,256]{2,0,1:T(1,128)} %get-tuple-element.739) | copy-start | bytes 15364
  828.8 40.7 %copy-start.47 = (f32[1,5,256]{2,0,1:T(1,128)S(1)}, f32[1,5,256]{2,0,1:T(1,128)}, u32[]{:S(2)}) copy-start(f32[1,5,256]{2,0,1:T(1,128)} %get-tuple-element.740) | copy-start | bytes 15364
  828.9 41.9 %copy-start.14 = (f32[5,768]{1,0:T(8,128)S(1)}, f32[5,768]{1,0:T(8,128)}, u32[]{:S(2)}) copy-start(f32[5,768]{1,0:T(8,128)} %copy-done.13) | copy-start | bytes 46084
  828.9 41.9 %copy-start.29 = (f32[1,6,768]{2,0,1:T(1,128)S(1)}, f32[1,6,768]{2,0,1:T(1,128)}, u32[]{:S(2)}) copy-start(f32[1,6,768]{2,0,1:T(1,128)} %get-tuple-element.729) | copy-start | bytes 55300
  828.9 41.9 %copy-start.30 = (f32[1,6,768]{2,0,1:T(1,128)S(1)}, f32[1,6,768]{2,0,1:T(1,128)}, u32[]{:S(2)}) copy-start(f32[1,6,768]{2,0,1:T(1,128)} %get-tuple-element.730) | copy-start | bytes 55300
  828.9 43.2 %copy-start.41 = (f32[1536]{0:T(1024)S(1)}, f32[1536]{0:T(1024)}, u32[]{:S(2)}) copy-start(f32[1536]{0:T(1024)} %get-tuple-element.612) | copy-start | bytes 18436
  828.9 43.2 %copy-start.42 = (f32[1536]{0:T(1024)S(1)}, f32[1536]{0:T(1024)}, u32[]{:S(2)}) copy-start(f32[1536]{0:T(1024)} %get-tuple-element.613) | copy-start | bytes 18436
  828.9 43.1 %copy-start.44 = (f32[1536]{0:T(1024)S(1)}, f32[1536]{0:T(1024)}, u32[]{:S(2)}) copy-start(f32[1536]{0:T(1024)} %param.26) | copy-start | bytes 18436
  (27 other events, 72.0 us)
Sparse Core Ops, SparseCore 0:
  9.6 66.1 all-gather.7
  78.3 37.4 all-gather.9
  118.2 28.8 all-gather.11
  148.6 63.6 all-gather.13
  336.9 33.8 reduce-scatter.11
  374.2 33.8 reduce-scatter.15
  410.5 34.4 all-reduce.32
  448.9 42.0 reduce-scatter.13
  494.5 53.7 reduce-scatter.9
  549.6 218.1 all-gather.15
  770.2 58.5 reduce-scatter.7
